TPU v7x, 32 devices: a whole 2x2x4 slice. The times are simulated.
32 devices in a mesh: row: 4 (over x, core), col: 8 (over z, y).
Axes of the slice: x: 2, y: 2, z: 4, core: 2. Of those that a mesh axis runs over, the one named last changes fastest.
Arguments:
- trailing: float32 [4096, 4096], P('row', 'col'), may hold values from -6 to 6
- panel_left: float32 [4096, 384], P(('row', 'col')), may hold values from -0.3125 to 0.3125
- panel_right: float32 [8, 1024, 384], P('row', 'col'), may hold values from -1 to 1
- panel_solved: float32 [1024, 1024], P('row', 'col'), may hold values from -1.75 to 1.75
- right_sides: float32 [4096, 1024], P('row', 'col'), may hold values from -6 to 6
- tile_ranks: int32 [8], replicated, may hold values from 64 to 384, as said below
- tile_order: int32 [8], replicated, may hold values from 0 to 7, each once
Outputs:
- trail_new: float32 [4096, 4096], P('row', 'col')
- rhs_new: float32 [4096, 1024], P('row', 'col')
Inputs may be any that keep to these rules, and one draw needn't show every extreme that they name: `tile_ranks`: every rank is a multiple of 64; both 64 and 384 occur in every draw. `tile_order`: each tile appears in exactly one slot.
All inputs are finite; a program needn't handle non-finite values.
Results may differ from a plain program's by a relative error of at most 0.00008.
Values sent between devices are 32-bit elements; how exact they have to be, the bound alone decides.
A program may use at most 64 MiB of HBM per device.

v0:
```python
import jax
import jax.numpy as jnp
from jax import lax
from jax.sharding import PartitionSpec as P


def spread(value, axis, root):
    mine = lax.axis_index(axis) == root
    return lax.psum(jnp.where(mine, value, jnp.zeros_like(value)), axis)


def exact_dot(left, right):
    return jnp.dot(left, right, precision=lax.Precision.HIGHEST, preferred_element_type=jnp.float32)


def on_device(trailing, panel_left, panel_right, panel_solved, right_sides, tile_ranks, tile_order):
    slot_count = panel_right.shape[0]
    tile_count = tile_order.shape[0]
    rank_width = panel_left.shape[1]
    left_rows, right_rows = (
        lax.all_gather(panel_left, "col", axis=0, tiled=True),
        lax.all_gather(panel_right, "col", axis=1, tiled=True),
    )
    tile_rows = left_rows.shape[0] // slot_count
    left_rows = left_rows.reshape(slot_count, tile_rows, rank_width)
    row_index = lax.axis_index("row")
    column = lax.axis_index("col")
    places = jnp.arange(tile_count, dtype=jnp.int32)
    levels = jnp.arange(rank_width, dtype=jnp.int32)
    slot_ids = row_index * slot_count + jnp.arange(slot_count, dtype=jnp.int32)
    my_tiles = jnp.sum(
        jnp.where(places[None, :] == slot_ids[:, None], tile_order[None, :], 0), axis=1
    )
    my_ranks = jnp.sum(
        jnp.where(places[None, :] == my_tiles[:, None], tile_ranks[None, :], 0), axis=1
    )
    keep_mask = (levels[None, :] < my_ranks[:, None]).astype(jnp.float32)
    left_mine = left_rows * keep_mask[:, None, :]
    root_slot = jnp.sum(jnp.where(tile_order == column, places, 0))
    root_row = root_slot // slot_count
    local_slot = root_slot % slot_count
    column_rank = jnp.sum(jnp.where(places == column, tile_ranks, 0))
    column_mask = (levels < column_rank).astype(jnp.float32)
    left_pick = (
        lax.dynamic_index_in_dim(left_rows, local_slot, 0, keepdims=False) * column_mask[None, :]
    )
    right_pick = lax.dynamic_index_in_dim(right_rows, local_slot, 0, keepdims=False)

    def owner_panel():
        return exact_dot(right_pick, left_pick.T)

    def other_panel():
        return jnp.zeros((right_pick.shape[0], tile_rows), jnp.float32)

    column_dense = lax.cond(row_index == root_row, owner_panel, other_panel)
    column_dense = spread(column_dense, "row", root_row)
    solved = jnp.einsum(
        "snk,nj->skj",
        right_rows,
        lax.all_gather(panel_solved, "row", axis=0, tiled=True),
        precision=lax.Precision.HIGHEST,
        preferred_element_type=jnp.float32,
    )
    updates = []
    for slot in range(slot_count):
        left_part = left_mine[slot]
        slot_right_part = right_rows[slot]
        middle = exact_dot(slot_right_part.T, column_dense)
        updates.append(exact_dot(left_part, jnp.concatenate([middle, solved[slot]], 1)))
    update_all = jnp.concatenate(updates, 0)
    trail_new = trailing - update_all[:, :tile_rows]
    rhs_new = right_sides - update_all[:, tile_rows:]
    return (trail_new, rhs_new)


def solution(mesh):
    return jax.shard_map(
        on_device,
        mesh=mesh,
        in_specs=(
            P("row", "col"),
            P(("row", "col"), None),
            P("row", "col", None),
            P("row", "col"),
            P("row", "col"),
            P(),
            P(),
        ),
        out_specs=(P("row", "col"), P("row", "col")),
        check_vma=False,
    )
```

profile of v0, /device:TPU:0, one launch (start us, length us, event | category | flops | bytes accessed | tf_op | source)
XLA Modules:
  0.0 198.6 jit_solution(3108771299947774375)
XLA Ops:
  7.2 0.7 all-gather.3.cloned.1.call-update
  7.9 0.7 all-gather.5.cloned.1.call-update
  8.7 1.3 fusion.27
  12.6 1.0 copy.10
  13.6 1.3 fusion.28
  14.9 0.6 compare_convert_fusion
  15.6 0.8 fusion.25
  16.4 0.8 fusion.26
  17.3 39.8 %all-gather.3.cloned.1.call-done = f32[1024,384]{1,0:T(8,128)} async-done(((f32[128,384]{1,0:T(8,128)}), f32[1024,384]{1,0:T(8,128)}) %all-gather.3.cloned.1.call-update) | async-done | bytes 1572880 | tf_op jit(solution)/shard_map/all_gather | solution.py:21
  57.1 60.6 %all-gather.5.cloned.1.call-done = f32[2,1024,384]{2,1,0:T(8,128)} async-done(((f32[2,128,384]{2,1,0:T(8,128)}), f32[2,1024,384]{2,1,0:T(8,128)}) %all-gather.5.cloned.1.call-update) | async-done | bytes 3145744 | tf_op jit(solution)/shard_map/all_gather | solution.py:22
  117.7 0.3 conditional.1
  117.7 0.2 broadcast.35
  118.0 1.5 broadcast_select_fusion
  119.5 12.9 %all_gather.11 = f32[1024,128]{0,1:T(8,128)S(1)} all-gather(f32[256,128]{0,1:T(8,128)S(1)} %copy.10), channel_id=1, replica_groups=mesh['row'=4,'col'=8] {'row'}, dimensions={0}, use_global_device_ids=true | all-gather | bytes 655360 | tf_op jit(solution)/shard_map/all_gather | solution.py:60
  132.4 2.7 %broadcast_multiply_fusion = f32[2,512,384]{2,1,0:T(8,128)} fusion(f32[2,512,384]{2,1,0:T(8,128)} %bitcast.38, f32[2,384]{1,0:T(2,128)S(1)} %compare_convert_fusion.1), kind=kLoop, calls=%fused_computation.29 | loop fusion | flops 393216 | bytes 3148800 | tf_op jit(solution)/shard_map/mul | solution.py:38
  135.1 1.9 fusion.23
  137.1 37.5 %all-reduce.2.cloned.1.call-done = f32[1024,512]{1,0:T(8,128)} async-done(((f32[1024,512]{1,0:T(8,128)}), f32[1024,512]{1,0:T(8,128)}) %all-reduce.2.cloned.1.call-update) | async-done | bytes 2097168 | tf_op jit(solution)/shard_map/psum | solution.py:9
  174.5 5.2 %fusion.13 = f32[384,512]{0,1:T(8,128)S(1)} fusion(f32[1024,512]{1,0:T(8,128)} %all-reduce.2.cloned.1.call-done, f32[2,1024,384]{2,1,0:T(8,128)S(1)} %copy-done), kind=kOutput, calls=%fused_computation.17 | convolution fusion | flops 2415919104 | bytes 4456448 | tf_op jit(solution)/shard_map/dot_general | solution.py:13
  179.7 2.5 %fusion.18 = f32[512,640]{1,0:T(8,128)S(1)} fusion(f32[384,128]{0,1:T(8,128)S(1)} %get-tuple-element.85, f32[384,512]{0,1:T(8,128)S(1)} %fusion.13, f32[2,512,384]{2,1,0:T(8,128)S(1)} %copy-done.2), kind=kOutput, calls=%fused_computation.23 | convolution fusion | flops 1510195200 | bytes 3080192 | tf_op jit(solution)/shard_map/dot_general | solution.py:13
  182.3 3.8 %fusion.12 = f32[384,512]{0,1:T(8,128)S(1)} fusion(f32[1024,512]{1,0:T(8,128)S(1)} %copy-done.1, f32[2,1024,384]{2,1,0:T(8,128)S(1)} %copy-done), kind=kOutput, calls=%fused_computation.16 | convolution fusion | flops 2415919104 | bytes 4456448 | tf_op jit(solution)/shard_map/dot_general | solution.py:13
  186.1 2.5 %fusion.14 = f32[512,640]{1,0:T(8,128)S(1)} fusion(f32[384,128]{0,1:T(8,128)S(1)} %get-tuple-element.86, f32[384,512]{0,1:T(8,128)S(1)} %fusion.12, f32[2,512,384]{2,1,0:T(8,128)S(1)} %copy-done.2), kind=kOutput, calls=%fused_computation.19 | convolution fusion | flops 1510195200 | bytes 3080192 | tf_op jit(solution)/shard_map/dot_general | solution.py:13
  188.6 0.9 fusion.22
  189.5 0.9 copy-done.3
  190.4 1.6 fusion.9
  (16 shorter events, 0.3 us)
Async XLA Ops:
  7.2 49.9 %all-gather.3.cloned.1.call-start = ((), (), s32[]{:S(2)}) async-start(), calls=%async_computation | async-start | bytes 1769472 | tf_op jit(solution)/shard_map/all_gather | solution.py:21
  7.9 109.8 %all-gather.5.cloned.1.call-start = ((), (), s32[]{:S(2)}) async-start(), calls=%async_computation.1 | async-start | bytes 3538944 | tf_op jit(solution)/shard_map/all_gather | solution.py:22
  8.6 165.9 %all-reduce.2.cloned.1.call-start = ((), (), s32[]{:S(2)}) async-start(), calls=%async_computation.2 | async-start | bytes 4194304 | tf_op jit(solution)/shard_map/psum | solution.py:9
  119.5 15.6 %copy-start = (f32[2,1024,384]{2,1,0:T(8,128)S(1)}, f32[2,1024,384]{2,1,0:T(8,128)}, u32[]{:S(2)}) copy-start(f32[2,1024,384]{2,1,0:T(8,128)} %all-gather.5.cloned.1.call-done) | copy-start | bytes 9437188
  174.5 5.2 %copy-start.2 = (f32[2,512,384]{2,1,0:T(8,128)S(1)}, f32[2,512,384]{2,1,0:T(8,128)}, u32[]{:S(2)}) copy-start(f32[2,512,384]{2,1,0:T(8,128)} %broadcast_multiply_fusion) | copy-start | bytes 4718596
  179.7 2.5 %copy-start.1 = (f32[1024,512]{1,0:T(8,128)S(1)}, f32[1024,512]{1,0:T(8,128)}, u32[]{:S(2)}) copy-start(f32[1024,512]{1,0:T(8,128)} %all-reduce.2.cloned.1.call-done) | copy-start | bytes 6291460
  186.1 2.5 %copy-start.4 = (f32[1024,128]{1,0:T(8,128)S(1)}, f32[1024,128]{1,0:T(8,128)}, u32[]{:S(2)}) copy-start(f32[1024,128]{1,0:T(8,128)} %param.13) | copy-start | bytes 1572868
  188.6 1.8 copy-start.3
Sparse Core Ops, SparseCore 0:
  10.2 46.8 all-gather.2
  59.3 58.3 all-gather.4
  120.6 53.8 all-reduce.1
where the time goes:
time: 199 us
  waiting for transfers between devices  139 us (70%)
  between operations  16.5 us (8%)
  matrix products  15.9 us (8%)
  blocking collectives  12.9 us (6%)
  other arithmetic  11.7 us (6%)
  local copies, waits for them, and re-layouts  2.21 us (1%)
    all_gather x1, waiting for transfers between devices, on_device(): lax.all_gather(panel_right, 'col', axis=1, tiled=True)  60.6 us
    all_gather x1, waiting for transfers between devices, on_device(): lax.all_gather(panel_left, 'col', axis=0, tiled=True)  39.8 us
    psum x1, waiting for transfers between devices, spread(): return lax.psum(jnp.where(mine, value, jnp.zeros_like(value)), axis)  37.5 us
    dot_general x4, matrix products, exact_dot(): jnp.dot(left, right, precision=lax.Precision.HIGHEST, preferred_element_t...  14 us
    all_gather x1, blocking collectives, on_device(): lax.all_gather(panel_solved, 'row', axis=0, tiled=True)  12.9 us
  transfers between devices with their start and end apart: 3, of which 3 were waited for; matrix products, arithmetic and copies ran while one was open for 5% of the time, Pallas kernels for 0%

commit v1 on v0

--- a/solution.py
+++ b/solution.py
@@ -2,6 +2,22 @@
 import jax.numpy as jnp
 from jax import lax
 from jax.sharding import PartitionSpec as P
+
+
+def product_in_turn(x, axis, dim, contribution):
+    length, index, span = (lax.axis_size(axis), lax.axis_index(axis), x.shape[dim])
+    ahead = [(i, (i + 1) % length) for i in range(length)]
+    downward = [(i, (i - 1) % length) for i in range(length)]
+    half = length // 2
+    from_left = from_right = x
+    subtotal = contribution(x, index * span)
+    for step in range(1, half + 1):
+        from_left = lax.ppermute(from_left, axis, ahead)
+        if step < length - half:
+            from_right = lax.ppermute(from_right, axis, downward)
+            subtotal = subtotal + contribution(from_right, (index + step) % length * span)
+        subtotal = subtotal + contribution(from_left, (index - step) % length * span)
+    return subtotal
 
 
 def spread(value, axis, root):
@@ -54,12 +70,17 @@
 
     column_dense = lax.cond(row_index == root_row, owner_panel, other_panel)
     column_dense = spread(column_dense, "row", root_row)
-    solved = jnp.einsum(
-        "snk,nj->skj",
-        right_rows,
-        lax.all_gather(panel_solved, "row", axis=0, tiled=True),
-        precision=lax.Precision.HIGHEST,
-        preferred_element_type=jnp.float32,
+    solved = product_in_turn(
+        panel_solved,
+        "row",
+        0,
+        lambda own_block, offset: jnp.einsum(
+            "snk,nj->skj",
+            lax.dynamic_slice_in_dim(right_rows, offset, own_block.shape[0], axis=1),
+            own_block,
+            precision=lax.Precision.HIGHEST,
+            preferred_element_type=jnp.float32,
+        ),
     )
     updates = []
     for slot in range(slot_count):

time: 199 us -> 202 us (1.015)
  blocking collectives: 12.9 us -> 0 us
  waiting for transfers between devices: 139 us -> 147 us
  local copies, waits for them, and re-layouts: 2.21 us -> 5.39 us
  starting transfers between devices: 0.11 us -> 3.25 us
    psum x1, waiting for transfers between devices: 37.5 us -> 52.2 us  [spread(): return lax.psum(jnp.where(mine, value, jnp.zeros_like(value)), axis)]
    all_gather x1 -> x0, blocking collectives: 12.9 us -> none  [on_device(): lax.all_gather(panel_solved, 'row', axis=0, tiled=True)]
    all_gather x1, waiting for transfers between devices: 39.8 us -> 35.9 us  [on_device(): lax.all_gather(panel_left, 'col', axis=0, tiled=True)]
    unnamed x11 -> x15, local copies, waits for them, and re-layouts: 1.93 us -> 5.11 us
    ppermute x0 -> x3, starting transfers between devices: none -> 3.14 us  [the longest x1 2.41 us: product_in_turn(): from_right = lax.ppermute(from_right, axis, downward)]
    all_gather x1, waiting for transfers between devices: 60.6 us -> 57.9 us  [on_device(): lax.all_gather(panel_right, 'col', axis=1, tiled=True)]
  transfers between devices with their start and end apart: 3 -> 6, of which waited for: 3 -> 3; matrix products, arithmetic and copies ran while one was open for 5% -> 7% of each run, Pallas kernels for 0% -> 0%
where the time goes in v1:
time: 202 us
  waiting for transfers between devices  147 us (73%)
  matrix products  17.3 us (9%)
  between operations  16.6 us (8%)
  other arithmetic  11.8 us (6%)
  local copies, waits for them, and re-layouts  5.39 us (3%)
  starting transfers between devices  3.25 us (2%)
    all_gather x1, waiting for transfers between devices, on_device(): lax.all_gather(panel_right, 'col', axis=1, tiled=True)  57.9 us
    psum x1, waiting for transfers between devices, spread(): return lax.psum(jnp.where(mine, value, jnp.zeros_like(value)), axis)  52.2 us
    all_gather x1, waiting for transfers between devices, on_device(): lax.all_gather(panel_left, 'col', axis=0, tiled=True)  35.9 us
    dot_general x4, matrix products, exact_dot(): jnp.dot(left, right, precision=lax.Precision.HIGHEST, preferred_element_t...  14 us
    unnamed x15, local copies, waits for them, and re-layouts  5.11 us
  transfers between devices with their start and end apart: 6, of which 3 were waited for; matrix products, arithmetic and copies ran while one was open for 7% of the time, Pallas kernels for 0%

profile of v1, /device:TPU:0, one launch (start us, length us, event | category | flops | bytes accessed | tf_op | source)
XLA Modules:
  0.0 201.8 jit_solution(6392189754128476521)
XLA Ops:
  7.2 0.7 all-gather.3.cloned.1.call-update
  7.9 0.7 all-gather.5.cloned.1.call-update
  8.7 1.7 copy.13
  10.4 2.4 %collective-permute-start = (f32[256,128]{0,1:T(8,128)}, f32[256,128]{0,1:T(8,128)S(1)}, u32[]{:S(2)}, u32[]{:S(2)}) collective-permute-start(f32[256,128]{0,1:T(8,128)} %copy.13), channel_id=1, source_target_pairs={{0,24},{8,0},{16,8},{24,16},{1,25},{9,1},{17,9},{25,17},{2,26},{10... | collective-permute-start | bytes 393224 | tf_op jit(solution)/shard_map/ppermute | solution.py:17
  12.8 1.3 fusion.38
  14.1 0.8 fusion.32
  14.9 0.8 fusion.33
  15.8 1.4 fusion.39
  20.5 0.7 collective-permute-start.2
  21.2 35.9 %all-gather.3.cloned.1.call-done = f32[1024,384]{1,0:T(8,128)} async-done(((f32[128,384]{1,0:T(8,128)}), f32[1024,384]{1,0:T(8,128)}) %all-gather.3.cloned.1.call-update) | async-done | bytes 1572880 | tf_op jit(solution)/shard_map/all_gather | solution.py:37
  57.1 2.7 %broadcast_multiply_fusion = f32[2,512,384]{2,1,0:T(8,128)} fusion(f32[2,512,384]{2,1,0:T(8,128)} %bitcast.45, f32[2,384]{1,0:T(2,128)S(1)} %compare_convert_fusion.1), kind=kLoop, calls=%fused_computation.37 | loop fusion | flops 393216 | bytes 3148800 | tf_op jit(solution)/shard_map/mul | solution.py:54
  59.8 57.9 %all-gather.5.cloned.1.call-done = f32[2,1024,384]{2,1,0:T(8,128)} async-done(((f32[2,128,384]{2,1,0:T(8,128)}), f32[2,1024,384]{2,1,0:T(8,128)}) %all-gather.5.cloned.1.call-update) | async-done | bytes 3145744 | tf_op jit(solution)/shard_map/all_gather | solution.py:38
  118.2 1.3 copy-done.2
  119.5 1.5 broadcast_select_fusion
  121.0 1.1 copy-done
  124.1 1.5 convolution_add_fusion
  125.6 52.2 %all-reduce.2.cloned.1.call-done = f32[1024,512]{1,0:T(8,128)} async-done(((f32[1024,512]{1,0:T(8,128)}), f32[1024,512]{1,0:T(8,128)}) %all-reduce.2.cloned.1.call-update) | async-done | bytes 2097168 | tf_op jit(solution)/shard_map/psum | solution.py:25
  177.8 5.2 %fusion.13 = f32[384,512]{0,1:T(8,128)S(1)} fusion(f32[1024,512]{1,0:T(8,128)} %all-reduce.2.cloned.1.call-done, f32[2,1024,384]{2,1,0:T(8,128)S(1)} %copy-done), kind=kOutput, calls=%fused_computation.17 | convolution fusion | flops 2415919104 | bytes 4456448 | tf_op jit(solution)/shard_map/dot_general | solution.py:29
  183.0 2.5 %fusion.18 = f32[512,640]{1,0:T(8,128)S(1)} fusion(f32[384,128]{0,1:T(8,128)S(1)} %get-tuple-element.85, f32[384,512]{0,1:T(8,128)S(1)} %fusion.13, f32[2,512,384]{2,1,0:T(8,128)S(1)} %copy-done.3), kind=kOutput, calls=%fused_computation.26 | convolution fusion | flops 1510195200 | bytes 3080192 | tf_op jit(solution)/shard_map/dot_general | solution.py:29
  185.5 3.8 %fusion.12 = f32[384,512]{0,1:T(8,128)S(1)} fusion(f32[1024,512]{1,0:T(8,128)S(1)} %copy-done.1, f32[2,1024,384]{2,1,0:T(8,128)S(1)} %copy-done), kind=kOutput, calls=%fused_computation.16 | convolution fusion | flops 2415919104 | bytes 4456448 | tf_op jit(solution)/shard_map/dot_general | solution.py:29
  189.3 2.5 %fusion.14 = f32[512,640]{1,0:T(8,128)S(1)} fusion(f32[384,128]{0,1:T(8,128)S(1)} %get-tuple-element.86, f32[384,512]{0,1:T(8,128)S(1)} %fusion.12, f32[2,512,384]{2,1,0:T(8,128)S(1)} %copy-done.3), kind=kOutput, calls=%fused_computation.22 | convolution fusion | flops 1510195200 | bytes 3080192 | tf_op jit(solution)/shard_map/dot_general | solution.py:29
  191.9 0.9 fusion.27
  192.7 0.9 copy-done.4
  193.6 1.6 fusion.9
  (28 shorter events, 3.5 us)
Async XLA Ops:
  7.2 49.9 %all-gather.3.cloned.1.call-start = ((), (), s32[]{:S(2)}) async-start(), calls=%async_computation | async-start | bytes 1769472 | tf_op jit(solution)/shard_map/all_gather | solution.py:37
  7.9 109.8 %all-gather.5.cloned.1.call-start = ((), (), s32[]{:S(2)}) async-start(), calls=%async_computation.1 | async-start | bytes 3538944 | tf_op jit(solution)/shard_map/all_gather | solution.py:38
  8.6 169.1 %all-reduce.2.cloned.1.call-start = ((), (), s32[]{:S(2)}) async-start(), calls=%async_computation.2 | async-start | bytes 4194304 | tf_op jit(solution)/shard_map/psum | solution.py:25
  10.4 112.5 %collective-permute-start = (f32[256,128]{0,1:T(8,128)}, f32[256,128]{0,1:T(8,128)S(1)}, u32[]{:S(2)}, u32[]{:S(2)}) collective-permute-start(f32[256,128]{0,1:T(8,128)} %copy.13), channel_id=1, source_target_pairs={{0,24},{8,0},{16,8},{24,16},{1,25},{9,1},{17,9},{25,17},{2,26},{10... | collective-permute-start | bytes 393224 | tf_op jit(solution)/shard_map/ppermute | solution.py:17
  12.8 7.7 %collective-permute-start.1 = (f32[256,128]{0,1:T(8,128)}, f32[256,128]{0,1:T(8,128)S(1)}, u32[]{:S(2)}, u32[]{:S(2)}) collective-permute-start(f32[256,128]{0,1:T(8,128)} %copy.13), channel_id=1, source_target_pairs={{0,8},{8,16},{16,24},{24,0},{1,9},{9,17},{17,25},{25,1},{2,10},{10... | collective-permute-start | bytes 393224 | tf_op jit(solution)/shard_map/ppermute | solution.py:15
  20.5 103.6 %collective-permute-start.2 = (f32[256,128]{0,1:T(8,128)S(1)}, f32[256,128]{0,1:T(8,128)}, u32[]{:S(2)}, u32[]{:S(2)}) collective-permute-start(f32[256,128]{0,1:T(8,128)S(1)} %collective-permute-done.1), channel_id=1, source_target_pairs={{0,8},{8,16},{16,24},{24,0},{1,9},{9,17},{17,25},{25,1},{2,10},{10... | collective-permute-start | bytes 393224 | tf_op jit(solution)/shard_map/ppermute | solution.py:15
  118.1 1.3 copy-start.2
  119.5 2.6 %copy-start = (f32[2,1024,384]{2,1,0:T(8,128)S(1)}, f32[2,1024,384]{2,1,0:T(8,128)}, u32[]{:S(2)}) copy-start(f32[2,1024,384]{2,1,0:T(8,128)} %all-gather.5.cloned.1.call-done) | copy-start | bytes 9437188
  121.0 1.2 copy-start.6
  177.8 5.2 %copy-start.3 = (f32[2,512,384]{2,1,0:T(8,128)S(1)}, f32[2,512,384]{2,1,0:T(8,128)}, u32[]{:S(2)}) copy-start(f32[2,512,384]{2,1,0:T(8,128)} %broadcast_multiply_fusion) | copy-start | bytes 4718596
  183.0 2.5 %copy-start.1 = (f32[1024,512]{1,0:T(8,128)S(1)}, f32[1024,512]{1,0:T(8,128)}, u32[]{:S(2)}) copy-start(f32[1024,512]{1,0:T(8,128)} %all-reduce.2.cloned.1.call-done) | copy-start | bytes 6291460
  189.3 2.5 %copy-start.5 = (f32[1024,128]{1,0:T(8,128)S(1)}, f32[1024,128]{1,0:T(8,128)}, u32[]{:S(2)}) copy-start(f32[1024,128]{1,0:T(8,128)} %param.13) | copy-start | bytes 1572868
  191.9 1.8 copy-start.4
Sparse Core Ops, SparseCore 0:
  10.2 46.8 all-gather.2
  59.3 58.3 all-gather.4
  121.2 56.5 all-reduce.1
